TPU v7x, 32 devices: a whole 2x2x4 slice. The times are simulated.
32 devices in a mesh: context: 4 (over z), tensor: 2 (over core), dp: 4 (over y, x).
Axes of the slice: x: 2, y: 2, z: 4, core: 2. Of those that a mesh axis runs over, the one named last changes fastest.
Arguments:
- queries: bfloat16 [4, 3072, 2048], P('dp', 'context', 'tensor'), may hold values from -1.75 to 1.75
- keys_in: bfloat16 [4, 3072, 2048], P('dp', 'context', 'tensor'), may hold values from -1.75 to 1.75
- values: bfloat16 [4, 3072, 2048], P('dp', 'context', 'tensor'), may hold values from -48 to 48
- norm_gain: float32 [2048], P('tensor'), may hold values from 0.25 to 1.75
- segment_ids: int32 [4, 48], P('dp', 'context'), may hold values from 0 to 5, never falling along the last dimension, each value on 1 to 24 neighbouring positions
- grad_out: bfloat16 [4, 3072, 2048], P('dp', 'context', 'tensor'), may hold values from -8 to 8
Outputs:
- normed_out: bfloat16 [4, 3072, 2048], P('dp', 'context', 'tensor')
- grad_queries: bfloat16 [4, 3072, 2048], P('dp', 'context', 'tensor')
- grad_keys: bfloat16 [4, 3072, 2048], P('dp', 'context', 'tensor')
- grad_values: bfloat16 [4, 3072, 2048], P('dp', 'context', 'tensor')
- grad_gain: float32 [2048], P('tensor')
Inputs may be any that keep to these rules, and one draw needn't show every extreme that they name: `segment_ids`: along each sequence the ids never fall; each id is one document.
All inputs are finite; a program needn't handle non-finite values.
Results may differ from a plain program's by a relative error of at most 0.0057.
Values sent between devices are 32-bit elements; how exact they have to be, the bound alone decides.
A program may use at most 128 MiB of HBM per device.

v0:
```python
import jax
import jax.numpy as jnp
from jax import lax
from jax.sharding import PartitionSpec as P

HD = 128
BLK = 256
SEGB = 64
WIDTH = 2048


def shifted(block, axis, distance):
    devices = range(lax.axis_size(axis))
    route = [(i - distance, i) for i in devices if i - distance in devices]
    return lax.ppermute(block, axis, route)


def prefix(value, axis, combine, identity):
    size, place = (lax.axis_size(axis), lax.axis_index(axis))
    everything = jax.tree.map(lambda part: lax.all_gather(part, axis), value)
    start = jax.tree.map(
        lambda part, zero: jnp.broadcast_to(jnp.asarray(zero, part.dtype), part.shape),
        value,
        identity,
    )

    def step(k, before):
        at = size - 1 - k
        reached = at > place
        new = combine(before, jax.tree.map(lambda part: part[at], everything))
        return jax.tree.map(lambda a, b: jnp.where(reached, a, b), new, before)

    return lax.fori_loop(0, size, step, start)


def join_forward(earlier, later):
    early_state, early_segs = earlier
    late_state, late_segs = later
    matches = jnp.logical_or(
        jnp.logical_and(early_segs[1] == late_segs[0], late_segs[0] == late_segs[1]),
        late_segs[0] == 0.0,
    )
    joined = late_state + jnp.where(matches, early_state, 0.0)
    first_seg = jnp.where(early_segs[0] == 0.0, late_segs[0], early_segs[0])
    last_seg = jnp.where(late_segs[1] == 0.0, early_segs[1], late_segs[1])
    return (joined, jnp.stack([first_seg, last_seg]))


def join_backward(earlier, later):
    high_state, high_segs = earlier
    low_state, low_segs = later
    matches = jnp.logical_or(
        jnp.logical_and(high_segs[0] == low_segs[1], low_segs[0] == low_segs[1]), low_segs[0] == 0.0
    )
    joined = low_state + jnp.where(matches, high_state, 0.0)
    first_seg = jnp.where(low_segs[0] == 0.0, high_segs[0], low_segs[0])
    last_seg = jnp.where(high_segs[1] == 0.0, low_segs[1], high_segs[1])
    return (joined, jnp.stack([first_seg, last_seg]))


def block_mask(seg_block):
    length = seg_block.shape[0]
    row_index = lax.broadcasted_iota(jnp.int32, (length, length), 0)
    col_index = lax.broadcasted_iota(jnp.int32, (length, length), 1)
    return jnp.logical_and(row_index >= col_index, seg_block[:, None] == seg_block[None, :])


def forward_block(carried, block_in):
    kv_state, seg_prev = carried
    q_block, k_block, v_block, seg_block = block_in
    visible = block_mask(seg_block)
    scores = jnp.einsum("thd,shd->hts", q_block, k_block, preferred_element_type=jnp.float32)
    weights = jnp.where(visible[None], scores, 0.0).astype(jnp.bfloat16)
    intra = jnp.einsum("hts,she->the", weights, v_block, preferred_element_type=jnp.float32)
    state_bf = kv_state.astype(jnp.bfloat16)
    inter = jnp.einsum("thd,hde->the", q_block, state_bf, preferred_element_type=jnp.float32)
    matches = (seg_block == seg_prev)[:, None, None]
    attended = intra + jnp.where(matches, inter, 0.0)
    last_seg = seg_block[-1]
    in_last = (seg_block == last_seg)[:, None, None]
    added = jnp.einsum(
        "thd,the->hde",
        jnp.where(in_last, k_block, jnp.zeros_like(k_block)),
        v_block,
        preferred_element_type=jnp.float32,
    )
    new_state = jnp.where(seg_prev == last_seg, kv_state, 0.0) + added
    return ((new_state, last_seg), (attended, weights, state_bf, seg_prev))


def backward_block(grad_state, block_in):
    q_block, k_block, v_block, seg_block, grad_block, weights, state_bf, seg_prev = block_in
    visible = block_mask(seg_block)
    grad_scores = jnp.einsum(
        "the,she->hts", grad_block, v_block, preferred_element_type=jnp.float32
    )
    grad_weights = jnp.where(visible[None], grad_scores, 0.0).astype(jnp.bfloat16)
    grad_bf = grad_state.astype(jnp.bfloat16)
    before = (seg_block == seg_prev)[:, None, None]
    after = (seg_block == seg_block[-1])[:, None, None]
    grad_q = jnp.einsum("hts,shd->thd", grad_weights, k_block, preferred_element_type=jnp.float32)
    grad_q = grad_q + jnp.where(
        before,
        jnp.einsum("the,hde->thd", grad_block, state_bf, preferred_element_type=jnp.float32),
        0.0,
    )
    grad_k = jnp.einsum("hts,thd->shd", grad_weights, q_block, preferred_element_type=jnp.float32)
    grad_k = grad_k + jnp.where(
        after, jnp.einsum("she,hde->shd", v_block, grad_bf, preferred_element_type=jnp.float32), 0.0
    )
    grad_v = jnp.einsum("hts,the->she", weights, grad_block, preferred_element_type=jnp.float32)
    grad_v = grad_v + jnp.where(
        after, jnp.einsum("shd,hde->she", k_block, grad_bf, preferred_element_type=jnp.float32), 0.0
    )
    added = jnp.einsum(
        "thd,the->hde",
        jnp.where(before, q_block, jnp.zeros_like(q_block)),
        grad_block,
        preferred_element_type=jnp.float32,
    )
    new_grad = jnp.where(seg_prev == seg_block[-1], grad_state, 0.0) + added
    return (
        new_grad,
        (grad_q.astype(jnp.bfloat16), grad_k.astype(jnp.bfloat16), grad_v.astype(jnp.bfloat16)),
    )


def body(queries, keys_in, values, norm_gain, segment_ids, grad_out):
    tok_count = queries.shape[1]
    local_width = queries.shape[2]
    head_count = local_width // HD
    block_count = tok_count // BLK
    seg_tok = jnp.repeat(segment_ids[0], SEGB)
    seg_blocks = seg_tok.reshape(block_count, BLK)
    flat_q = queries[0].reshape(tok_count, head_count, HD)
    flat_k = keys_in[0].reshape(tok_count, head_count, HD)
    flat_v = values[0].reshape(tok_count, head_count, HD)
    first_seg = seg_tok[0]
    last_seg = seg_tok[-1]
    own_segs = jnp.stack([first_seg + 1, last_seg + 1]).astype(jnp.float32)
    in_last = (seg_tok == last_seg)[:, None, None]
    own_kv = jnp.einsum(
        "thd,the->hde",
        jnp.where(in_last, flat_k, jnp.zeros_like(flat_k)),
        flat_v,
        preferred_element_type=jnp.float32,
    )
    empty = (jnp.zeros_like(own_kv), jnp.zeros((2,), jnp.float32))

    def relay_step(step_index, incoming):
        return shifted(join_forward(incoming, (own_kv, own_segs)), "context", 1)

    arrived = lax.fori_loop(0, lax.axis_size("context") - 1, relay_step, empty)
    state_in = jnp.where(arrived[1][1] == own_segs[0], arrived[0], 0.0)
    block_q = flat_q.reshape(block_count, BLK, head_count, HD)
    block_k = flat_k.reshape(block_count, BLK, head_count, HD)
    block_v = flat_v.reshape(block_count, BLK, head_count, HD)
    final, stored = lax.scan(
        forward_block, (state_in, first_seg), (block_q, block_k, block_v, seg_blocks)
    )
    attended_blocks, weights_all, state_all, prev_all = stored
    attended = attended_blocks.reshape(tok_count, local_width)
    cotangent = grad_out[0].astype(jnp.float32)
    gained = cotangent * norm_gain
    squares, inner = lax.psum(
        (jnp.sum(attended * attended, axis=1), jnp.sum(gained * attended, axis=1)), "tensor"
    )
    radius = jnp.sqrt(squares / WIDTH + 1e-06)
    normed = attended / radius[:, None]
    normed_out = (normed * norm_gain).astype(jnp.bfloat16)
    grad_gain = lax.psum(jnp.sum(cotangent * normed, axis=0), ("context", "dp"))
    grad_att = (
        (gained - attended * (inner / (WIDTH * radius * radius))[:, None]) / radius[:, None]
    ).astype(jnp.bfloat16)
    flat_da = grad_att.reshape(tok_count, head_count, HD)
    in_first = (seg_tok == first_seg)[:, None, None]
    own_grad = jnp.einsum(
        "thd,the->hde",
        jnp.where(in_first, flat_q, jnp.zeros_like(flat_q)),
        flat_da,
        preferred_element_type=jnp.float32,
    )
    behind = prefix((own_grad, own_segs), "context", join_backward, empty)
    grad_in = jnp.where(behind[1][0] == own_segs[1], behind[0], 0.0)
    block_da = flat_da.reshape(block_count, BLK, head_count, HD)
    leftover, grads = lax.scan(
        backward_block,
        grad_in,
        (block_q, block_k, block_v, seg_blocks, block_da, weights_all, state_all, prev_all),
        reverse=True,
    )
    grad_queries = grads[0].reshape(1, tok_count, local_width)
    grad_keys = grads[1].reshape(1, tok_count, local_width)
    grad_values = grads[2].reshape(1, tok_count, local_width)
    return (
        normed_out.reshape(1, tok_count, local_width),
        grad_queries,
        grad_keys,
        grad_values,
        grad_gain,
    )


def solution(mesh):
    in_specs = (
        P("dp", "context", "tensor"),
        P("dp", "context", "tensor"),
        P("dp", "context", "tensor"),
        P("tensor"),
        P("dp", "context"),
        P("dp", "context", "tensor"),
    )
    out_specs = (
        P("dp", "context", "tensor"),
        P("dp", "context", "tensor"),
        P("dp", "context", "tensor"),
        P("dp", "context", "tensor"),
        P("tensor"),
    )
    return jax.shard_map(body, mesh=mesh, in_specs=in_specs, out_specs=out_specs, check_vma=False)
```

profile of v0, /device:TPU:0, one launch (start us, length us, event | category | flops | bytes accessed | tf_op | source)
XLA Modules:
  0.0 330.4 jit_solution(14289737301600793897)
XLA Ops:
  20.1 50.7 %while.71 = (s32[]{:T(128)}, f32[8,128,128]{2,1,0:T(8,128)S(1)}, f32[2]{0:T(128)S(1)}, f32[2]{0:T(128)S(1)}, pred[]{:T(512)}, /*index=5*/pred[]{:T(512)}, f32[8,...) while((s32[]{:T(128)}, f32[8,128,128]{2,1,0:T(8,128)S(1)}, f32[2]{0:T(128)S(1)}, f32[2]{0:T(128)S(1)}, ...), condition=%wide.region_1.2_spmd, body=%wide.region_0.1_spmd.sunk | while | flops 262154 | bytes 3670328 | solution.py:153
  22.2 5.0 %collective-permute-start = (f32[8,128,128]{2,1,0:T(8,128)S(1)}, f32[8,128,128]{2,1,0:T(8,128)S(1)}, u32[]{:S(2)}, u32[]{:S(2)}) collective-permute-start(f32[8,128,128]{2,1,0:T(8,128)S(1)} %select_add_fusion.2), channel_id=1, source_target_pairs={{0,8},{8,16},{16,24},{1,9},{9,17},{17,25},{2,10},{10,18},{18,26},{... | collective-permute-start | bytes 1572872 | tf_op jit(solution)/shard_map/while/body/eval_jaxpr/ppermute | solution.py:15
  30.5 3.4 %collective-permute-start.1 = (f32[2]{0:T(128)S(1)}, f32[2]{0:T(128)S(1)}, u32[]{:S(2)}, u32[]{:S(2)}) collective-permute-start(f32[2]{0:T(128)S(1)} %pad_maximum_fusion.2), channel_id=1, source_target_pairs={{0,8},{8,16},{16,24},{1,9},{9,17},{17,25},{2,10},{10,18},{18,26},{... | collective-permute-start | bytes 32 | tf_op jit(solution)/shard_map/while/body/eval_jaxpr/ppermute | solution.py:15
  33.9 4.4 %collective-permute-done.1 = f32[2]{0:T(128)S(1)} collective-permute-done((f32[2]{0:T(128)S(1)}, f32[2]{0:T(128)S(1)}, u32[]{:S(2)}, u32[]{:S(2)}) %collective-permute-start.1) | collective-permute-done | bytes 40 | tf_op jit(solution)/shard_map/while/body/eval_jaxpr/ppermute | solution.py:15
  40.4 4.4 %collective-permute-start = (f32[8,128,128]{2,1,0:T(8,128)S(1)}, f32[8,128,128]{2,1,0:T(8,128)S(1)}, u32[]{:S(2)}, u32[]{:S(2)}) collective-permute-start(f32[8,128,128]{2,1,0:T(8,128)S(1)} %select_add_fusion.2), channel_id=1, source_target_pairs={{0,8},{8,16},{16,24},{1,9},{9,17},{17,25},{2,10},{10,18},{18,26},{... | collective-permute-start | bytes 1572872 | tf_op jit(solution)/shard_map/while/body/eval_jaxpr/ppermute | solution.py:15
  48.2 3.4 %collective-permute-start.1 = (f32[2]{0:T(128)S(1)}, f32[2]{0:T(128)S(1)}, u32[]{:S(2)}, u32[]{:S(2)}) collective-permute-start(f32[2]{0:T(128)S(1)} %pad_maximum_fusion.2), channel_id=1, source_target_pairs={{0,8},{8,16},{16,24},{1,9},{9,17},{17,25},{2,10},{10,18},{18,26},{... | collective-permute-start | bytes 32 | tf_op jit(solution)/shard_map/while/body/eval_jaxpr/ppermute | solution.py:15
  51.6 3.5 %collective-permute-done.1 = f32[2]{0:T(128)S(1)} collective-permute-done((f32[2]{0:T(128)S(1)}, f32[2]{0:T(128)S(1)}, u32[]{:S(2)}, u32[]{:S(2)}) %collective-permute-start.1) | collective-permute-done | bytes 40 | tf_op jit(solution)/shard_map/while/body/eval_jaxpr/ppermute | solution.py:15
  57.2 4.4 %collective-permute-start = (f32[8,128,128]{2,1,0:T(8,128)S(1)}, f32[8,128,128]{2,1,0:T(8,128)S(1)}, u32[]{:S(2)}, u32[]{:S(2)}) collective-permute-start(f32[8,128,128]{2,1,0:T(8,128)S(1)} %select_add_fusion.2), channel_id=1, source_target_pairs={{0,8},{8,16},{16,24},{1,9},{9,17},{17,25},{2,10},{10,18},{18,26},{... | collective-permute-start | bytes 1572872 | tf_op jit(solution)/shard_map/while/body/eval_jaxpr/ppermute | solution.py:15
  64.9 3.4 %collective-permute-start.1 = (f32[2]{0:T(128)S(1)}, f32[2]{0:T(128)S(1)}, u32[]{:S(2)}, u32[]{:S(2)}) collective-permute-start(f32[2]{0:T(128)S(1)} %pad_maximum_fusion.2), channel_id=1, source_target_pairs={{0,8},{8,16},{16,24},{1,9},{9,17},{17,25},{2,10},{10,18},{18,26},{... | collective-permute-start | bytes 32 | tf_op jit(solution)/shard_map/while/body/eval_jaxpr/ppermute | solution.py:15
  74.2 3.1 copy.106
  80.4 31.8 %while.72 = (s32[]{:T(128)}, f32[8,128,128]{2,1,0:T(8,128)S(1)}, s32[]{:T(128)}, f32[3,256,8,128]{1,3,2,0:T(8,128)}, bf16[3,8,256,256]{3,2,1,0:T(8,128)(2,1)}, /...) while((s32[]{:T(128)}, f32[8,128,128]{2,1,0:T(8,128)S(1)}, ...), condition=%wide.region_3.4_spmd, body=%wide.region_2.3_spmd.sunk | while | flops 405209600 | bytes 18224672 | solution.py:158
  113.4 2.5 copy.70
  118.1 2.6 copy.93
  128.9 4.9 %fusion.54 = bf16[768,8,128]{2,1,0:T(8,128)(2,1)S(1)} fusion(f32[96,8,8,128]{3,2,1,0:T(8,128)} %copy-done.6, f32[3,256,8,128]{3,2,1,0:T(8,128)S(1)} %copy.70, f32[768]{0:T(1024)S(1)} %get-tuple-element.728, f32[768]{0:T(1024)S(1)} %get-tuple-element.727, f32[8,128]{1,0:T(8,128)S(1)} %bitcast.320), kind=kLoop, calls=%fused_computation.98 | loop fusion | flops 3932160 | bytes 7874560 | tf_op jit(solution)/shard_map/convert_element_type | solution.py:174
  135.3 12.0 %all-gather.1 = f32[4,1,2]{2,1,0:T(1,128)S(1)} all-gather(f32[1,1,2]{2,1,0:T(1,128)S(1)} %fusion.66), channel_id=1, replica_groups=mesh['context'=4,'tensor'=2,'dp'=4] {'context'}, dimensions={0}, use_global_device_ids=true | all-gather | bytes 40 | tf_op jit(solution)/shard_map/all_gather | solution.py:20
  152.2 39.9 %psum.23 = f32[1024]{0:T(1024)} all-reduce(f32[1024]{0:T(1024)S(1)} %fusion.51), channel_id=1, replica_groups=mesh['context'=4,'tensor'=2,'dp'=4] {'context','dp'}, use_global_device_ids=true, to_apply=%region_13.14 | all-reduce | flops 1024 | bytes 8192 | tf_op jit(solution)/shard_map/psum | solution.py:171
  192.2 3.7 %multiply_convert_fusion = bf16[1,768,1024]{2,1,0:T(8,128)(2,1)} fusion(f32[1,768,1024]{2,1,0:T(8,128)} %reshape.302, f32[1024]{0:T(1024)S(1)} %copy-done.15, f32[768]{0:T(1024)S(1)} %get-tuple-element.728), kind=kLoop, calls=%fused_computation.102 | loop fusion | flops 2359296 | bytes 4725760 | tf_op jit(solution)/shard_map/convert_element_type | solution.py:170
  195.9 2.9 divide_convert_fusion
  198.8 39.5 %while.74 = (s32[]{:T(128)}, f32[8,128,128]{2,1,0:T(8,128)}, f32[2]{0:T(128)S(1)}, s32[]{:T(128)}, f32[4,8,128,128]{3,2,1,0:T(8,128)}, /*index=5*/f32[4,2]{0,1:T...) while((s32[]{:T(128)}, f32[8,128,128]{2,1,0:T(8,128)}, ...), condition=%wide.region_9.10_spmd.clone, body=%wide.region_8.9_spmd.clone.sunk | while | flops 524312 | bytes 1573215 | solution.py:33
  244.1 71.5 %while.73 = (s32[]{:T(128)}, f32[8,128,128]{2,1,0:T(8,128)S(1)}, bf16[3,256,8,128]{3,2,1,0:T(8,128)(2,1)}, bf16[3,256,8,128]{3,2,1,0:T(8,128)(2,1)}, bf16[3,256,...) while((s32[]{:T(128)}, f32[8,128,128]{2,1,0:T(8,128)S(1)}, ...), condition=%wide.region_11.12_spmd, body=%wide.region_10.11_spmd.sunk | while | flops 809697792 | bytes 39720800 | solution.py:186
  245.3 2.5 select_convert_fusion.3
  269.2 2.5 select_convert_fusion.3
  293.0 2.5 select_convert_fusion.3
  315.7 3.8 %reshape.304 = bf16[1,768,1024]{2,1,0:T(8,128)(2,1)} reshape(bf16[3,256,8,128]{3,2,1,0:T(8,128)(2,1)} %get-tuple-element.544) | data formatting | bytes 3145728 | tf_op jit(solution)/shard_map/reshape | solution.py:192
  (240 shorter events, 147.2 us)
Async XLA Ops:
  7.2 191.7 %all-gather.4.cloned.1.call-start = ((), (), s32[]{:S(2)}) async-start(), calls=%async_computation | async-start | bytes 2621440 | tf_op jit(solution)/shard_map/all_gather | solution.py:20
  14.4 2.0 copy-start.8
  16.4 1.7 copy-start.10
  20.1 53.1 %copy-start.16 = (s32[1,12]{1,0:T(1,128)S(1)}, s32[1,12]{1,0:T(1,128)}, u32[]{:S(2)}) copy-start(s32[1,12]{1,0:T(1,128)} %param.18) | copy-start | bytes 148
  22.2 16.1 %collective-permute-start = (f32[8,128,128]{2,1,0:T(8,128)S(1)}, f32[8,128,128]{2,1,0:T(8,128)S(1)}, u32[]{:S(2)}, u32[]{:S(2)}) collective-permute-start(f32[8,128,128]{2,1,0:T(8,128)S(1)} %select_add_fusion.2), channel_id=1, source_target_pairs={{0,8},{8,16},{16,24},{1,9},{9,17},{17,25},{2,10},{10,18},{18,26},{... | collective-permute-start | bytes 1572872 | tf_op jit(solution)/shard_map/while/body/eval_jaxpr/ppermute | solution.py:15
  30.5 7.9 %collective-permute-start.1 = (f32[2]{0:T(128)S(1)}, f32[2]{0:T(128)S(1)}, u32[]{:S(2)}, u32[]{:S(2)}) collective-permute-start(f32[2]{0:T(128)S(1)} %pad_maximum_fusion.2), channel_id=1, source_target_pairs={{0,8},{8,16},{16,24},{1,9},{9,17},{17,25},{2,10},{10,18},{18,26},{... | collective-permute-start | bytes 32 | tf_op jit(solution)/shard_map/while/body/eval_jaxpr/ppermute | solution.py:15
  40.4 14.7 %collective-permute-start = (f32[8,128,128]{2,1,0:T(8,128)S(1)}, f32[8,128,128]{2,1,0:T(8,128)S(1)}, u32[]{:S(2)}, u32[]{:S(2)}) collective-permute-start(f32[8,128,128]{2,1,0:T(8,128)S(1)} %select_add_fusion.2), channel_id=1, source_target_pairs={{0,8},{8,16},{16,24},{1,9},{9,17},{17,25},{2,10},{10,18},{18,26},{... | collective-permute-start | bytes 1572872 | tf_op jit(solution)/shard_map/while/body/eval_jaxpr/ppermute | solution.py:15
  48.2 6.9 %collective-permute-start.1 = (f32[2]{0:T(128)S(1)}, f32[2]{0:T(128)S(1)}, u32[]{:S(2)}, u32[]{:S(2)}) collective-permute-start(f32[2]{0:T(128)S(1)} %pad_maximum_fusion.2), channel_id=1, source_target_pairs={{0,8},{8,16},{16,24},{1,9},{9,17},{17,25},{2,10},{10,18},{18,26},{... | collective-permute-start | bytes 32 | tf_op jit(solution)/shard_map/while/body/eval_jaxpr/ppermute | solution.py:15
  57.2 13.7 %collective-permute-start = (f32[8,128,128]{2,1,0:T(8,128)S(1)}, f32[8,128,128]{2,1,0:T(8,128)S(1)}, u32[]{:S(2)}, u32[]{:S(2)}) collective-permute-start(f32[8,128,128]{2,1,0:T(8,128)S(1)} %select_add_fusion.2), channel_id=1, source_target_pairs={{0,8},{8,16},{16,24},{1,9},{9,17},{17,25},{2,10},{10,18},{18,26},{... | collective-permute-start | bytes 1572872 | tf_op jit(solution)/shard_map/while/body/eval_jaxpr/ppermute | solution.py:15
  64.9 5.9 %collective-permute-start.1 = (f32[2]{0:T(128)S(1)}, f32[2]{0:T(128)S(1)}, u32[]{:S(2)}, u32[]{:S(2)}) collective-permute-start(f32[2]{0:T(128)S(1)} %pad_maximum_fusion.2), channel_id=1, source_target_pairs={{0,8},{8,16},{16,24},{1,9},{9,17},{17,25},{2,10},{10,18},{18,26},{... | collective-permute-start | bytes 32 | tf_op jit(solution)/shard_map/while/body/eval_jaxpr/ppermute | solution.py:15
  74.2 3.1 copy-start.11
  82.4 1.6 copy-start.3
  93.0 1.6 copy-start.3
  103.6 1.6 copy-start.3
  103.6 1.6 copy-start.4
  122.5 2.4 copy-start.15
  123.3 1.7 copy-start.6
  128.9 4.9 %copy-start.14 = (bf16[1,768,1024]{1,2,0:T(8,128)(2,1)S(1)}, bf16[1,768,1024]{1,2,0:T(8,128)(2,1)}, u32[]{:S(2)}) copy-start(bf16[1,768,1024]{1,2,0:T(8,128)(2,1)} %copy.93) | copy-start | bytes 4718596
  192.2 3.7 %copy-start.7 = (f32[96,8,8,128]{3,2,1,0:T(8,128)S(1)}, f32[96,8,8,128]{3,2,1,0:T(8,128)}, u32[]{:S(2)}) copy-start(f32[96,8,8,128]{3,2,1,0:T(8,128)} %copy-done.6) | copy-start | bytes 9437188
  261.5 1.8 copy-start
  285.3 1.8 copy-start
  309.1 1.8 copy-start
  315.7 3.8 %copy-start.12 = (bf16[3,256,8,128]{3,2,1,0:T(8,128)(2,1)S(1)}, bf16[3,256,8,128]{3,2,1,0:T(8,128)(2,1)}, u32[]{:S(2)}) copy-start(bf16[3,256,8,128]{3,2,1,0:T(8,128)(2,1)} %get-tuple-element.545) | copy-start | bytes 4718596
  319.5 2.0 copy-start.13
  (10 other events, 13.9 us)
Sparse Core Ops, SparseCore 0:
  135.4 48.6 all-gather.3
where the time goes:
time: 334 us; the launch traced here: 330 us
  local copies, waits for them, and re-layouts  78.9 us (24%)
  blocking collectives  54.4 us (16%)
  matrix products  54.3 us (16%)
  loops' own time  48.1 us (14%)
  other arithmetic  40.1 us (12%)
  starting transfers between devices  24.2 us (7%)
  between operations  20 us (6%)
  waiting for transfers between devices  10.4 us (3%)
    psum x1, blocking collectives, body(): grad_gain = lax.psum(jnp.sum(cotangent * normed, axis=0), ('context', 'dp'))  39.9 us
    another operation x1, loops' own time, prefix(): return lax.fori_loop(0, size, step, start)  25.8 us
    ppermute x6, starting transfers between devices, shifted(): return lax.ppermute(block, axis, route)  24.2 us
    dynamic_slice x24, local copies, waits for them, and re-layouts, body(): lax.scan(forward_block, (state_in, first_seg), (block_q, block_k, block_v...  20.9 us
    another operation x1, loops' own time, body(): arrived = lax.fori_loop(0, lax.axis_size('context') - 1, relay_step, empty)  13.8 us
    all_gather x1, blocking collectives, prefix(): everything = jax.tree.map(lambda part: lax.all_gather(part, axis), value)  12 us
    unnamed x29, local copies, waits for them, and re-layouts  11.9 us
    ppermute x6, waiting for transfers between devices, shifted(): return lax.ppermute(block, axis, route)  10.4 us
  transfers between devices with their start and end apart: 7, of which 3 were waited for; matrix products, arithmetic and copies ran while one was open for 4% of the time, Pallas kernels for 0%

commit v1 on v0

--- a/solution.py
+++ b/solution.py
@@ -168,7 +168,7 @@
     radius = jnp.sqrt(squares / WIDTH + 1e-06)
     normed = attended / radius[:, None]
     normed_out = (normed * norm_gain).astype(jnp.bfloat16)
-    grad_gain = lax.psum(jnp.sum(cotangent * normed, axis=0), ("context", "dp"))
+    grad_gain = lax.psum(lax.psum(jnp.sum(cotangent * normed, axis=0), "dp"), "context")
     grad_att = (
         (gained - attended * (inner / (WIDTH * radius * radius))[:, None]) / radius[:, None]
     ).astype(jnp.bfloat16)

time: 334 us -> 317 us (0.949)
  blocking collectives: 54.4 us -> 33.9 us
  waiting for transfers between devices: 10.4 us -> 15.9 us
    psum x1 -> x2, blocking collectives: 39.9 us -> 19.4 us  [the longest x1 9.89 us: body(): lax.psum(jnp.sum(cotangent * normed, axis=0), 'dp')]
    all_gather x1, waiting for transfers between devices: 0.01 us -> 5.47 us  [prefix(): everything = jax.tree.map(lambda part: lax.all_gather(part, axis), value)]
  transfers between devices with their start and end apart: 7 -> 7, of which waited for: 3 -> 4; matrix products, arithmetic and copies ran while one was open for 4% -> 4% of each run, Pallas kernels for 0% -> 0%
where the time goes in v1:
time: 317 us; the launch traced here: 314 us
  local copies, waits for them, and re-layouts  78.8 us (25%)
  matrix products  54.3 us (17%)
  loops' own time  47 us (15%)
  other arithmetic  40.1 us (13%)
  blocking collectives  33.9 us (11%)
  starting transfers between devices  24.2 us (8%)
  between operations  19.9 us (6%)
  waiting for transfers between devices  15.9 us (5%)
    another operation x1, loops' own time, prefix(): return lax.fori_loop(0, size, step, start)  24.6 us
    ppermute x6, starting transfers between devices, shifted(): return lax.ppermute(block, axis, route)  24.2 us
    dynamic_slice x24, local copies, waits for them, and re-layouts, body(): lax.scan(forward_block, (state_in, first_seg), (block_q, block_k, block_v...  20.9 us
    another operation x1, loops' own time, body(): arrived = lax.fori_loop(0, lax.axis_size('context') - 1, relay_step, empty)  14 us
    all_gather x1, blocking collectives, prefix(): everything = jax.tree.map(lambda part: lax.all_gather(part, axis), value)  12 us
    unnamed x29, local copies, waits for them, and re-layouts  11.9 us
    ppermute x6, waiting for transfers between devices, shifted(): return lax.ppermute(block, axis, route)  10.4 us
    psum x1, blocking collectives, body(): lax.psum(jnp.sum(cotangent * normed, axis=0), 'dp')  9.89 us
  transfers between devices with their start and end apart: 7, of which 4 were waited for; matrix products, arithmetic and copies ran while one was open for 4% of the time, Pallas kernels for 0%

profile of v1, /device:TPU:0, one launch (start us, length us, event | category | flops | bytes accessed | tf_op | source)
XLA Modules:
  0.0 314.1 jit_solution(10235065618864790981)
XLA Ops:
  20.0 50.9 %while.71 = (s32[]{:T(128)}, f32[8,128,128]{2,1,0:T(8,128)S(1)}, f32[2]{0:T(128)S(1)}, f32[2]{0:T(128)S(1)}, pred[]{:T(512)}, /*index=5*/pred[]{:T(512)}, f32[8,...) while((s32[]{:T(128)}, f32[8,128,128]{2,1,0:T(8,128)S(1)}, f32[2]{0:T(128)S(1)}, f32[2]{0:T(128)S(1)}, ...), condition=%wide.region_1.2_spmd, body=%wide.region_0.1_spmd.sunk | while | flops 262154 | bytes 3670328 | solution.py:153
  22.2 5.0 %collective-permute-start = (f32[8,128,128]{2,1,0:T(8,128)S(1)}, f32[8,128,128]{2,1,0:T(8,128)S(1)}, u32[]{:S(2)}, u32[]{:S(2)}) collective-permute-start(f32[8,128,128]{2,1,0:T(8,128)S(1)} %select_add_fusion.2), channel_id=1, source_target_pairs={{0,8},{8,16},{16,24},{1,9},{9,17},{17,25},{2,10},{10,18},{18,26},{... | collective-permute-start | bytes 1572872 | tf_op jit(solution)/shard_map/while/body/eval_jaxpr/ppermute | solution.py:15
  30.5 3.4 %collective-permute-start.1 = (f32[2]{0:T(128)S(1)}, f32[2]{0:T(128)S(1)}, u32[]{:S(2)}, u32[]{:S(2)}) collective-permute-start(f32[2]{0:T(128)S(1)} %pad_maximum_fusion.2), channel_id=1, source_target_pairs={{0,8},{8,16},{16,24},{1,9},{9,17},{17,25},{2,10},{10,18},{18,26},{... | collective-permute-start | bytes 32 | tf_op jit(solution)/shard_map/while/body/eval_jaxpr/ppermute | solution.py:15
  33.9 4.4 %collective-permute-done.1 = f32[2]{0:T(128)S(1)} collective-permute-done((f32[2]{0:T(128)S(1)}, f32[2]{0:T(128)S(1)}, u32[]{:S(2)}, u32[]{:S(2)}) %collective-permute-start.1) | collective-permute-done | bytes 40 | tf_op jit(solution)/shard_map/while/body/eval_jaxpr/ppermute | solution.py:15
  40.5 4.4 %collective-permute-start = (f32[8,128,128]{2,1,0:T(8,128)S(1)}, f32[8,128,128]{2,1,0:T(8,128)S(1)}, u32[]{:S(2)}, u32[]{:S(2)}) collective-permute-start(f32[8,128,128]{2,1,0:T(8,128)S(1)} %select_add_fusion.2), channel_id=1, source_target_pairs={{0,8},{8,16},{16,24},{1,9},{9,17},{17,25},{2,10},{10,18},{18,26},{... | collective-permute-start | bytes 1572872 | tf_op jit(solution)/shard_map/while/body/eval_jaxpr/ppermute | solution.py:15
  48.2 3.4 %collective-permute-start.1 = (f32[2]{0:T(128)S(1)}, f32[2]{0:T(128)S(1)}, u32[]{:S(2)}, u32[]{:S(2)}) collective-permute-start(f32[2]{0:T(128)S(1)} %pad_maximum_fusion.2), channel_id=1, source_target_pairs={{0,8},{8,16},{16,24},{1,9},{9,17},{17,25},{2,10},{10,18},{18,26},{... | collective-permute-start | bytes 32 | tf_op jit(solution)/shard_map/while/body/eval_jaxpr/ppermute | solution.py:15
  51.7 3.5 %collective-permute-done.1 = f32[2]{0:T(128)S(1)} collective-permute-done((f32[2]{0:T(128)S(1)}, f32[2]{0:T(128)S(1)}, u32[]{:S(2)}, u32[]{:S(2)}) %collective-permute-start.1) | collective-permute-done | bytes 40 | tf_op jit(solution)/shard_map/while/body/eval_jaxpr/ppermute | solution.py:15
  57.3 4.4 %collective-permute-start = (f32[8,128,128]{2,1,0:T(8,128)S(1)}, f32[8,128,128]{2,1,0:T(8,128)S(1)}, u32[]{:S(2)}, u32[]{:S(2)}) collective-permute-start(f32[8,128,128]{2,1,0:T(8,128)S(1)} %select_add_fusion.2), channel_id=1, source_target_pairs={{0,8},{8,16},{16,24},{1,9},{9,17},{17,25},{2,10},{10,18},{18,26},{... | collective-permute-start | bytes 1572872 | tf_op jit(solution)/shard_map/while/body/eval_jaxpr/ppermute | solution.py:15
  65.0 3.4 %collective-permute-start.1 = (f32[2]{0:T(128)S(1)}, f32[2]{0:T(128)S(1)}, u32[]{:S(2)}, u32[]{:S(2)}) collective-permute-start(f32[2]{0:T(128)S(1)} %pad_maximum_fusion.2), channel_id=1, source_target_pairs={{0,8},{8,16},{16,24},{1,9},{9,17},{17,25},{2,10},{10,18},{18,26},{... | collective-permute-start | bytes 32 | tf_op jit(solution)/shard_map/while/body/eval_jaxpr/ppermute | solution.py:15
  74.3 3.1 copy.106
  80.5 32.1 %while.72 = (s32[]{:T(128)}, f32[8,128,128]{2,1,0:T(8,128)S(1)}, s32[]{:T(128)}, f32[3,256,8,128]{1,3,2,0:T(8,128)}, bf16[3,8,256,256]{3,2,1,0:T(8,128)(2,1)}, /...) while((s32[]{:T(128)}, f32[8,128,128]{2,1,0:T(8,128)S(1)}, ...), condition=%wide.region_3.4_spmd, body=%wide.region_2.3_spmd.sunk | while | flops 405209600 | bytes 18224672 | solution.py:158
  113.8 2.5 copy.70
  118.5 2.6 copy.93
  129.3 4.9 %fusion.54 = bf16[768,8,128]{2,1,0:T(8,128)(2,1)S(1)} fusion(f32[96,8,8,128]{3,2,1,0:T(8,128)} %copy-done.6, f32[3,256,8,128]{3,2,1,0:T(8,128)S(1)} %copy.70, f32[768]{0:T(1024)S(1)} %get-tuple-element.728, f32[768]{0:T(1024)S(1)} %get-tuple-element.727, f32[8,128]{1,0:T(8,128)S(1)} %bitcast.320), kind=kLoop, calls=%fused_computation.98 | loop fusion | flops 3932160 | bytes 7874560 | tf_op jit(solution)/shard_map/convert_element_type | solution.py:174
  135.7 12.0 %all-gather.1 = f32[4,1,2]{2,1,0:T(1,128)S(1)} all-gather(f32[1,1,2]{2,1,0:T(1,128)S(1)} %fusion.66), channel_id=1, replica_groups=mesh['context'=4,'tensor'=2,'dp'=4] {'context'}, dimensions={0}, use_global_device_ids=true | all-gather | bytes 40 | tf_op jit(solution)/shard_map/all_gather | solution.py:20
  152.6 9.9 %psum.30 = f32[1024]{0:T(1024)S(1)} all-reduce(f32[1024]{0:T(1024)S(1)} %fusion.51), channel_id=1, replica_groups=mesh['context'=4,'tensor'=2,'dp'=4] {'dp'}, use_global_device_ids=true, to_apply=%region_13.14 | all-reduce | flops 1024 | bytes 8192 | tf_op jit(solution)/shard_map/psum | solution.py:171
  162.5 9.5 %psum.31 = f32[1024]{0:T(1024)} all-reduce(f32[1024]{0:T(1024)S(1)} %psum.30), channel_id=1, replica_groups=mesh['context'=4,'tensor'=2,'dp'=4] {'context'}, use_global_device_ids=true, to_apply=%region_14.15 | all-reduce | flops 1024 | bytes 8192 | tf_op jit(solution)/shard_map/psum | solution.py:171
  172.0 3.7 %multiply_convert_fusion = bf16[1,768,1024]{2,1,0:T(8,128)(2,1)} fusion(f32[1,768,1024]{2,1,0:T(8,128)} %reshape.302, f32[1024]{0:T(1024)S(1)} %copy-done.15, f32[768]{0:T(1024)S(1)} %get-tuple-element.728), kind=kLoop, calls=%fused_computation.102 | loop fusion | flops 2359296 | bytes 4725760 | tf_op jit(solution)/shard_map/convert_element_type | solution.py:170
  175.7 2.9 divide_convert_fusion
  178.7 5.5 %all-gather.4.cloned.1.call-done = f32[32,128,128]{2,1,0:T(8,128)} async-done(((f32[8,128,128]{2,1,0:T(8,128)}), f32[32,128,128]{2,1,0:T(8,128)}) %all-gather.4.cloned.1.call-update) | async-done | bytes 2097168 | tf_op jit(solution)/shard_map/all_gather | solution.py:20
  184.2 38.2 %while.74 = (s32[]{:T(128)}, f32[8,128,128]{2,1,0:T(8,128)}, f32[2]{0:T(128)S(1)}, s32[]{:T(128)}, f32[4,8,128,128]{3,2,1,0:T(8,128)}, /*index=5*/f32[4,2]{0,1:T...) while((s32[]{:T(128)}, f32[8,128,128]{2,1,0:T(8,128)}, ...), condition=%wide.region_9.10_spmd.clone, body=%wide.region_8.9_spmd.clone.sunk | while | flops 524312 | bytes 1573215 | solution.py:33
  228.1 71.2 %while.73 = (s32[]{:T(128)}, f32[8,128,128]{2,1,0:T(8,128)S(1)}, bf16[3,256,8,128]{3,2,1,0:T(8,128)(2,1)}, bf16[3,256,8,128]{3,2,1,0:T(8,128)(2,1)}, bf16[3,256,...) while((s32[]{:T(128)}, f32[8,128,128]{2,1,0:T(8,128)S(1)}, ...), condition=%wide.region_11.12_spmd, body=%wide.region_10.11_spmd.sunk | while | flops 809697792 | bytes 39720800 | solution.py:186
  229.3 2.5 select_convert_fusion.3
  299.4 3.8 %reshape.304 = bf16[1,768,1024]{2,1,0:T(8,128)(2,1)} reshape(bf16[3,256,8,128]{3,2,1,0:T(8,128)(2,1)} %get-tuple-element.544) | data formatting | bytes 3145728 | tf_op jit(solution)/shard_map/reshape | solution.py:192
  (241 shorter events, 152.2 us)
Async XLA Ops:
  7.2 177.0 %all-gather.4.cloned.1.call-start = ((), (), s32[]{:S(2)}) async-start(), calls=%async_computation | async-start | bytes 2621440 | tf_op jit(solution)/shard_map/all_gather | solution.py:20
  14.3 2.0 copy-start.8
  16.3 1.7 copy-start.10
  20.0 53.3 %copy-start.16 = (s32[1,12]{1,0:T(1,128)S(1)}, s32[1,12]{1,0:T(1,128)}, u32[]{:S(2)}) copy-start(s32[1,12]{1,0:T(1,128)} %param.18) | copy-start | bytes 148
  22.2 16.1 %collective-permute-start = (f32[8,128,128]{2,1,0:T(8,128)S(1)}, f32[8,128,128]{2,1,0:T(8,128)S(1)}, u32[]{:S(2)}, u32[]{:S(2)}) collective-permute-start(f32[8,128,128]{2,1,0:T(8,128)S(1)} %select_add_fusion.2), channel_id=1, source_target_pairs={{0,8},{8,16},{16,24},{1,9},{9,17},{17,25},{2,10},{10,18},{18,26},{... | collective-permute-start | bytes 1572872 | tf_op jit(solution)/shard_map/while/body/eval_jaxpr/ppermute | solution.py:15
  30.5 7.9 %collective-permute-start.1 = (f32[2]{0:T(128)S(1)}, f32[2]{0:T(128)S(1)}, u32[]{:S(2)}, u32[]{:S(2)}) collective-permute-start(f32[2]{0:T(128)S(1)} %pad_maximum_fusion.2), channel_id=1, source_target_pairs={{0,8},{8,16},{16,24},{1,9},{9,17},{17,25},{2,10},{10,18},{18,26},{... | collective-permute-start | bytes 32 | tf_op jit(solution)/shard_map/while/body/eval_jaxpr/ppermute | solution.py:15
  40.5 14.7 %collective-permute-start = (f32[8,128,128]{2,1,0:T(8,128)S(1)}, f32[8,128,128]{2,1,0:T(8,128)S(1)}, u32[]{:S(2)}, u32[]{:S(2)}) collective-permute-start(f32[8,128,128]{2,1,0:T(8,128)S(1)} %select_add_fusion.2), channel_id=1, source_target_pairs={{0,8},{8,16},{16,24},{1,9},{9,17},{17,25},{2,10},{10,18},{18,26},{... | collective-permute-start | bytes 1572872 | tf_op jit(solution)/shard_map/while/body/eval_jaxpr/ppermute | solution.py:15
  48.2 6.9 %collective-permute-start.1 = (f32[2]{0:T(128)S(1)}, f32[2]{0:T(128)S(1)}, u32[]{:S(2)}, u32[]{:S(2)}) collective-permute-start(f32[2]{0:T(128)S(1)} %pad_maximum_fusion.2), channel_id=1, source_target_pairs={{0,8},{8,16},{16,24},{1,9},{9,17},{17,25},{2,10},{10,18},{18,26},{... | collective-permute-start | bytes 32 | tf_op jit(solution)/shard_map/while/body/eval_jaxpr/ppermute | solution.py:15
  57.3 13.7 %collective-permute-start = (f32[8,128,128]{2,1,0:T(8,128)S(1)}, f32[8,128,128]{2,1,0:T(8,128)S(1)}, u32[]{:S(2)}, u32[]{:S(2)}) collective-permute-start(f32[8,128,128]{2,1,0:T(8,128)S(1)} %select_add_fusion.2), channel_id=1, source_target_pairs={{0,8},{8,16},{16,24},{1,9},{9,17},{17,25},{2,10},{10,18},{18,26},{... | collective-permute-start | bytes 1572872 | tf_op jit(solution)/shard_map/while/body/eval_jaxpr/ppermute | solution.py:15
  65.0 5.9 %collective-permute-start.1 = (f32[2]{0:T(128)S(1)}, f32[2]{0:T(128)S(1)}, u32[]{:S(2)}, u32[]{:S(2)}) collective-permute-start(f32[2]{0:T(128)S(1)} %pad_maximum_fusion.2), channel_id=1, source_target_pairs={{0,8},{8,16},{16,24},{1,9},{9,17},{17,25},{2,10},{10,18},{18,26},{... | collective-permute-start | bytes 32 | tf_op jit(solution)/shard_map/while/body/eval_jaxpr/ppermute | solution.py:15
  74.3 3.1 copy-start.11
  82.5 1.6 copy-start.3
  82.5 1.6 copy-start.4
  103.9 1.6 copy-start.3
  103.9 1.6 copy-start.4
  122.9 2.4 copy-start.15
  123.7 1.6 copy-start.6
  129.3 4.9 %copy-start.14 = (bf16[1,768,1024]{1,2,0:T(8,128)(2,1)S(1)}, bf16[1,768,1024]{1,2,0:T(8,128)(2,1)}, u32[]{:S(2)}) copy-start(bf16[1,768,1024]{1,2,0:T(8,128)(2,1)} %copy.93) | copy-start | bytes 4718596
  172.0 3.7 %copy-start.7 = (f32[96,8,8,128]{3,2,1,0:T(8,128)S(1)}, f32[96,8,8,128]{3,2,1,0:T(8,128)}, u32[]{:S(2)}) copy-start(f32[96,8,8,128]{3,2,1,0:T(8,128)} %copy-done.6) | copy-start | bytes 9437188
  245.4 1.8 copy-start
  269.2 1.8 copy-start
  292.9 1.8 copy-start
  299.3 3.8 %copy-start.12 = (bf16[3,256,8,128]{3,2,1,0:T(8,128)(2,1)S(1)}, bf16[3,256,8,128]{3,2,1,0:T(8,128)(2,1)}, u32[]{:S(2)}) copy-start(bf16[3,256,8,128]{3,2,1,0:T(8,128)(2,1)} %get-tuple-element.545) | copy-start | bytes 4718596
  303.2 2.0 copy-start.13
  (10 other events, 13.9 us)
Sparse Core Ops, SparseCore 0:
  135.8 48.3 all-gather.3
